TPU v7x, 32 devices: a whole 2x2x4 slice. The times are simulated.
32 devices in a mesh: dp: 4 (over y, x), ctx: 2 (over core), expert: 4 (over z).
Axes of the slice: x: 2, y: 2, z: 4, core: 2. Of those that a mesh axis runs over, the one named last changes fastest.
Arguments:
- tokens: bfloat16 [96, 200, 512], P(('dp', 'expert'), 'ctx'), may hold values from -6 to 6
- gain_one: float32 [512], replicated, may hold values from 0.1 to 1.9
- w_qkv: bfloat16 [512, 1536], replicated, may hold values from -0.25 to 0.25
- w_out: bfloat16 [512, 512], replicated, may hold values from -1 to 1
- gain_two: float32 [512], replicated, may hold values from 0.1 to 1.9
- w_router: bfloat16 [512, 4], replicated, may hold values from -0.1875 to 0.1875
- w_in: bfloat16 [4, 512, 2048], P('expert'), may hold values from -0.25 to 0.25
- w_back: bfloat16 [4, 2048, 512], P('expert'), may hold values from -0.25 to 0.25
- route_ids: int32 [16, 2, 6, 100, 2], P(('dp', 'expert'), 'ctx'), may hold values from 0 to 3, all different within a row; in each aligned block of 600 rows (0 to 599, 600 to 1199, ..., all dimensions but the last counted through in order) at most 600 rows name the same one
- key_mask: int32 [96, 200], P(('dp', 'expert')), may hold values from 0 to 1, as said below
- cotangent: bfloat16 [96, 200, 512], P(('dp', 'expert'), 'ctx'), may hold values from -6 to 6
Outputs:
- mixed: bfloat16 [96, 200, 512], P(('dp', 'expert'), 'ctx')
- grad_tokens: bfloat16 [96, 200, 512], P(('dp', 'expert'), 'ctx')
- grad_gain_one: float32 [512], replicated
- grad_qkv: float32 [512, 1536], replicated
- grad_out: float32 [512, 512], replicated
- grad_gain_two: float32 [512], replicated
- grad_router: float32 [512, 4], replicated
- grad_in: float32 [4, 512, 2048], P('expert')
- grad_back: float32 [4, 2048, 512], P('expert')
Inputs may be any that keep to these rules, and one draw needn't show every extreme that they name: Among the 600 tokens of one device (one aligned block of route_ids), at most 600 routes name the same expert, ; a token's two experts differ. `key_mask`: each image's mask is 1 on a first run of positions of length 150 to 200, then 0.
All inputs are finite; a program needn't handle non-finite values.
Results may differ from a plain program's by a relative error of at most 0.017.
Values may be sent and summed in bfloat16 or wider, within the bound.
No kernel may reach another device: no remote copies, remote signals or barrier semaphores. Data moves between devices by JAX's collectives and lax.ppermute only.
A program may use at most 192 MiB of HBM per device.

v0:
```python
import jax
import jax.numpy as jnp
from jax import lax
from jax.sharding import PartitionSpec as P

HEADS = 8
HEAD_DIM = 64
TOP = 2


def norm_rows(value, gain):
    center = value - jnp.mean(value, -1, keepdims=True)
    spread = jnp.mean(center * center, -1, keepdims=True)
    return center * lax.rsqrt(spread + 1e-06) * gain


def smooth_gelu(value):
    return 0.5 * value * (1.0 + jnp.tanh(0.7978845608 * (value + 0.044715 * value * value * value)))


def forward(tokens, gain_one, w_qkv, w_out, gain_two, w_router, w_in, w_back, flat_ids, live):
    nimg, half, width = tokens.shape
    count = nimg * half
    experts_all = w_router.shape[1]
    capacity = max(2, 2 * TOP * count // experts_all)
    x_rows = tokens.astype(jnp.float32).reshape(count, width)
    normed = norm_rows(x_rows, gain_one).astype(jnp.bfloat16)
    qkv = jnp.dot(normed, w_qkv, preferred_element_type=jnp.float32).astype(jnp.bfloat16)
    qkv = qkv.reshape(nimg, half, 3 * width)
    query = qkv[..., :width]
    keys_local = qkv[..., width : 2 * width]
    vals_local = qkv[..., 2 * width :]
    keys, vals = (
        lax.all_gather(keys_local, "ctx", axis=1, tiled=True),
        lax.all_gather(vals_local, "ctx", axis=1, tiled=True),
    )
    seq = keys.shape[1]
    query4 = query.reshape(nimg, half, HEADS, HEAD_DIM)
    keys4 = keys.reshape(nimg, seq, HEADS, HEAD_DIM)
    vals4 = vals.reshape(nimg, seq, HEADS, HEAD_DIM)
    scale = HEAD_DIM ** (-0.5)
    scores = (
        jnp.einsum("iqhc,ikhc->ihqk", query4, keys4, preferred_element_type=jnp.float32) * scale
    )
    open_keys = live[:, None, None, :]
    masked = jnp.where(open_keys, scores, -1000000000.0)
    topmost = jnp.max(masked, -1, keepdims=True)
    expo = jnp.where(open_keys, jnp.exp(masked - topmost), 0.0)
    probs = expo / jnp.sum(expo, -1, keepdims=True)
    probs_low = probs.astype(jnp.bfloat16)
    mix = jnp.einsum("ihqk,ikhc->iqhc", probs_low, vals4, preferred_element_type=jnp.float32)
    mix = mix.reshape(count, width).astype(jnp.bfloat16)
    mid = x_rows + jnp.dot(mix, w_out, preferred_element_type=jnp.float32)
    routed = norm_rows(mid, gain_two).astype(jnp.bfloat16)
    logits = jnp.dot(routed, w_router, preferred_element_type=jnp.float32)
    pick = flat_ids[:, :, None] == jnp.arange(experts_all, dtype=jnp.int32)[None, None, :]
    chosen = jnp.sum(jnp.where(pick, logits[:, None, :], 0.0), -1)
    expo_gate = jnp.exp(chosen)
    gates = expo_gate / jnp.sum(expo_gate, -1, keepdims=True)
    pair_ids = flat_ids.reshape(-1)
    hits = (pair_ids[:, None] == jnp.arange(experts_all, dtype=jnp.int32)[None, :]).astype(
        jnp.int32
    )
    before = jnp.cumsum(hits, 0) - hits
    slots = jnp.sum(before * hits, 1)
    where_rows = pair_ids * capacity + slots
    sent = jnp.repeat(routed, TOP, axis=0)
    buffer = jnp.zeros((experts_all * capacity, width), jnp.bfloat16).at[where_rows].set(sent)
    buffer = buffer.reshape(experts_all, capacity, width)
    arrived = lax.all_to_all(buffer, "expert", split_axis=0, concat_axis=1, tiled=True)
    pre = jnp.einsum("erd,edf->erf", arrived, w_in, preferred_element_type=jnp.float32)
    act = smooth_gelu(pre).astype(jnp.bfloat16)
    made = jnp.einsum("erf,efd->erd", act, w_back, preferred_element_type=jnp.float32).astype(
        jnp.bfloat16
    )
    returned = lax.all_to_all(made, "expert", split_axis=1, concat_axis=0, tiled=True)
    picked = returned.reshape(experts_all * capacity, width)[where_rows].reshape(count, TOP, width)
    output = mid + jnp.sum(gates[:, :, None] * picked.astype(jnp.float32), 1)
    return (
        x_rows,
        normed,
        query4,
        keys4,
        vals4,
        probs,
        probs_low,
        mix,
        mid,
        routed,
        pick,
        gates,
        where_rows,
        arrived,
        pre,
        act,
        picked,
        output,
        capacity,
    )


def shards(
    tokens, gain_one, w_qkv, w_out, gain_two, w_router, w_in, w_back, route_ids, key_mask, cotangent
):
    nimg, half, width = tokens.shape
    count = nimg * half
    experts_all = w_router.shape[1]
    flat_ids = route_ids.reshape(count, TOP)
    live = key_mask > 0
    state = forward(
        tokens, gain_one, w_qkv, w_out, gain_two, w_router, w_in, w_back, flat_ids, live
    )
    mixed = state[17].reshape(nimg, half, width).astype(jnp.bfloat16)
    state = forward(
        tokens, gain_one, w_qkv, w_out, gain_two, w_router, w_in, w_back, flat_ids, live
    )
    (
        x_rows,
        normed,
        query4,
        keys4,
        vals4,
        probs,
        probs_low,
        mix,
        mid,
        routed,
        pick,
        gates,
        where_rows,
        arrived,
        pre,
        act,
        picked,
        output,
        capacity,
    ) = state
    scale = HEAD_DIM ** (-0.5)
    high = lax.Precision.HIGHEST
    grad_y = cotangent.astype(jnp.float32).reshape(count, width)
    grad_gate = jnp.sum(grad_y[:, None, :] * picked.astype(jnp.float32), -1)
    d_out = (
        (gates[:, :, None] * grad_y[:, None, :]).astype(jnp.bfloat16).reshape(count * TOP, width)
    )
    grad_buffer = jnp.zeros((experts_all * capacity, width), jnp.bfloat16).at[where_rows].set(d_out)
    grad_buffer = grad_buffer.reshape(experts_all, capacity, width)
    grad_arrived = lax.all_to_all(grad_buffer, "expert", split_axis=0, concat_axis=1, tiled=True)
    d_act = jnp.einsum("erd,efd->erf", grad_arrived, w_back, preferred_element_type=jnp.float32)
    grad_back = jnp.einsum("erf,erd->efd", act, grad_arrived, preferred_element_type=jnp.float32)
    _, gelu_pull = jax.vjp(smooth_gelu, pre)
    d_pre = gelu_pull(d_act)[0].astype(jnp.bfloat16)
    grad_in = jnp.einsum("erd,erf->edf", arrived, d_pre, preferred_element_type=jnp.float32)
    d_in = jnp.einsum("erf,edf->erd", d_pre, w_in, preferred_element_type=jnp.float32).astype(
        jnp.bfloat16
    )
    grad_returned = lax.all_to_all(d_in, "expert", split_axis=1, concat_axis=0, tiled=True)
    grad_rows = grad_returned.reshape(experts_all * capacity, width)[where_rows].reshape(
        count, TOP, width
    )
    d_experts = jnp.sum(grad_rows.astype(jnp.float32), 1)
    d_chosen = gates * (grad_gate - jnp.sum(gates * grad_gate, -1, keepdims=True))
    d_logits = jnp.sum(jnp.where(pick, d_chosen[:, :, None], 0.0), 1)
    grad_router = jnp.dot(routed.astype(jnp.float32).T, d_logits, precision=high)
    d_routed = d_experts + jnp.dot(d_logits, w_router.astype(jnp.float32).T, precision=high)
    _, norm_two_pull = jax.vjp(norm_rows, mid, gain_two)
    d_mid_norm, grad_gain_two = norm_two_pull(d_routed)
    d_mid = grad_y + d_mid_norm
    d_branch = d_mid.astype(jnp.bfloat16)
    grad_out = jnp.einsum("td,te->de", mix, d_branch, preferred_element_type=jnp.float32)
    d_mix = jnp.dot(d_branch, w_out.T, preferred_element_type=jnp.float32).astype(jnp.bfloat16)
    d_mix4 = d_mix.reshape(nimg, half, HEADS, HEAD_DIM)
    d_probs = jnp.einsum("iqhc,ikhc->ihqk", d_mix4, vals4, preferred_element_type=jnp.float32)
    d_scores = (probs * (d_probs - jnp.sum(probs * d_probs, -1, keepdims=True))).astype(
        jnp.bfloat16
    )
    d_query = (
        jnp.einsum("ihqk,ikhc->iqhc", d_scores, keys4, preferred_element_type=jnp.float32) * scale
    )
    d_keys = (
        jnp.einsum("ihqk,iqhc->ikhc", d_scores, query4, preferred_element_type=jnp.float32) * scale
    )
    d_vals = jnp.einsum("ihqk,iqhc->ikhc", probs_low, d_mix4, preferred_element_type=jnp.float32)
    seq = keys4.shape[1]
    d_keys_own, d_vals_own = (
        lax.psum_scatter(
            d_keys.reshape(nimg, seq, width).astype(jnp.bfloat16),
            "ctx",
            scatter_dimension=1,
            tiled=True,
        ).astype(jnp.float32),
        lax.psum_scatter(
            d_vals.reshape(nimg, seq, width).astype(jnp.bfloat16),
            "ctx",
            scatter_dimension=1,
            tiled=True,
        ).astype(jnp.float32),
    )
    d_qkv = jnp.concatenate(
        [
            d_query.reshape(count, width).astype(jnp.bfloat16),
            d_keys_own.reshape(count, width).astype(jnp.bfloat16),
            d_vals_own.reshape(count, width).astype(jnp.bfloat16),
        ],
        axis=1,
    )
    grad_qkv = jnp.einsum("td,te->de", normed, d_qkv, preferred_element_type=jnp.float32)
    d_normed = jnp.dot(d_qkv, w_qkv.T, preferred_element_type=jnp.float32)
    _, norm_one_pull = jax.vjp(norm_rows, x_rows, gain_one)
    d_x_norm, grad_gain_one = norm_one_pull(d_normed)
    grad_tokens = (d_mid + d_x_norm).reshape(nimg, half, width).astype(jnp.bfloat16)
    grad_gain_one, grad_qkv, grad_out, grad_gain_two, grad_router = lax.psum(
        (grad_gain_one, grad_qkv, grad_out, grad_gain_two, grad_router), ("dp", "ctx", "expert")
    )
    grad_in, grad_back = (
        lax.psum(grad_in.astype(jnp.bfloat16), ("dp", "ctx")).astype(jnp.float32),
        lax.psum(grad_back.astype(jnp.bfloat16), ("dp", "ctx")).astype(jnp.float32),
    )
    return (
        mixed,
        grad_tokens,
        grad_gain_one,
        grad_qkv,
        grad_out,
        grad_gain_two,
        grad_router,
        grad_in,
        grad_back,
    )


def solution(mesh):
    placed = (
        P(("dp", "expert"), "ctx", None),
        P(),
        P(),
        P(),
        P(),
        P(),
        P("expert", None, None),
        P("expert", None, None),
        P(("dp", "expert"), "ctx", None, None, None),
        P(("dp", "expert"), None),
        P(("dp", "expert"), "ctx", None),
    )
    return jax.shard_map(
        shards,
        mesh=mesh,
        in_specs=placed,
        out_specs=(
            P(("dp", "expert"), "ctx", None),
            P(("dp", "expert"), "ctx", None),
            P(),
            P(),
            P(),
            P(),
            P(),
            P("expert", None, None),
            P("expert", None, None),
        ),
        check_vma=False,
    )
```

profile of v0, /device:TPU:0, one launch (start us, length us, event | category | flops | bytes accessed | tf_op | source)
XLA Modules:
  0.0 711.9 jit_solution(9703908839708034771)
XLA Ops:
  12.5 3.8 convolution_convert_fusion.2
  16.4 3.7 reshape.366
  31.7 4.3 mul.324
  36.1 4.0 copy.110
  40.1 6.3 fusion.48
  48.7 4.0 copy.107
  52.7 3.9 fusion.22
  64.7 14.4 %scatter_custom_fusion.1 = bf16[2400,512]{1,0:T(8,128)(2,1)} fusion(s32[1200]{0:T(1024)S(1)} %fusion.39, f32[1200,512]{1,0:T(8,128)} %mul.324, f32[1200]{0:T(1024)S(1)} %div.90, bf16[]{:T(256)} %constant.40.clone.1), kind=kCustom, calls=%fused_computation.58 | custom fusion | flops 1228800 | bytes 4923394 | tf_op jit(solution)/shard_map/scatter | solution.py:145
  79.0 4.9 all-to-all-start.2
  85.6 3.9 reshape.409
  89.5 10.2 %scatter_custom_fusion = bf16[2400,512]{1,0:T(8,128)(2,1)} fusion(s32[1200]{0:T(1024)S(1)} %fusion.39, bf16[1200,512]{1,0:T(8,128)(2,1)} %reshape.409, bf16[]{:T(256)} %constant.40.clone.1), kind=kCustom, calls=%fused_computation.68 | custom fusion | bytes 2458112 | tf_op jit(solution)/shard_map/scatter | solution.py:68
  99.7 40.7 %all-to-all-done.2 = bf16[4,600,512]{2,1,0:T(8,128)(2,1)} async-done(((bf16[4,600,512]{2,1,0:T(8,128)(2,1)}), bf16[4,600,512]{2,1,0:T(8,128)(2,1)}, u32[]{:S(2)}, u32[]{:S(2)}) %all-to-all-start.2) | async-done | bytes 2457632 | tf_op jit(solution)/shard_map/all_to_all | solution.py:147
  140.4 4.8 all-to-all-start
  145.2 11.4 %fusion.15 = f32[2400,2048]{1,0:T(8,128)} fusion(bf16[2400,512]{1,0:T(8,128)(2,1)} %bitcast.11, bf16[1,2048,512]{2,1,0:T(8,128)(2,1)} %param.18), kind=kOutput, calls=%fused_computation.40 | convolution fusion | flops 5033164800 | bytes 24215552 | tf_op jit(solution)/shard_map/erd,efd->erf/dot_general | solution.py:148
  156.6 44.1 %all-to-all-done = bf16[4,600,512]{2,1,0:T(8,128)(2,1)} async-done(((bf16[4,600,512]{2,1,0:T(8,128)(2,1)}), bf16[4,600,512]{2,1,0:T(8,128)(2,1)}, u32[]{:S(2)}, u32[]{:S(2)}) %all-to-all-start) | async-done | bytes 2457632 | tf_op jit(solution)/shard_map/all_to_all | solution.py:70
  200.8 24.4 %fusion.4 = (bf16[2400,2048]{1,0:T(8,128)(2,1)}, bf16[2400,2048]{1,0:T(8,128)(2,1)S(1)}) fusion(f32[2400,2048]{1,0:T(8,128)} %fusion.15, bf16[2400,512]{1,0:T(8,128)(2,1)} %bitcast.6, bf16[1,512,2048]{2,1,0:T(8,128)(2,1)S(1)} %copy-done), kind=kOutput, calls=%fused_computation.12 | convolution fusion | flops 5160960000 | bytes 43876352 | tf_op jit(solution)/shard_map/erd,edf->erf/dot_general | solution.py:71
  225.2 5.5 fusion.7
  230.7 21.7 %copy.149 = bf16[1,2400,512]{2,0,1:T(2,128)(2,1)} copy(bf16[1,2400,512]{2,1,0:T(8,128)(2,1)S(1)} %fusion.7) | data formatting | bytes 4915200 | tf_op jit(solution)/shard_map/convert_element_type | solution.py:73
  252.9 17.7 %reduce.11 = bf16[2400,512]{1,0:T(8,128)(2,1)} reduce(bf16[2400,1,512]{2,1,0:T(2,128)(2,1)} %bitcast.107, bf16[]{:T(256)} %broadcast.269), dimensions={1}, to_apply=%bitcast.101.reduce_sub_computation | reduce | bytes 4915202
  270.6 4.3 reshape.434
  274.9 4.9 all-to-all-start.1
  279.9 9.4 %fusion.8 = bf16[1,2400,512]{2,1,0:T(8,128)(2,1)S(1)} fusion(bf16[2400,2048]{1,0:T(8,128)(2,1)} %get-tuple-element.28, bf16[1,512,2048]{2,1,0:T(8,128)(2,1)S(1)} %copy-done), kind=kOutput, calls=%fused_computation.23 | convolution fusion | flops 5034393600 | bytes 14385152 | tf_op jit(solution)/shard_map/erf,edf->erd/dot_general | solution.py:153
  289.2 21.7 %copy.148 = bf16[1,2400,512]{2,0,1:T(2,128)(2,1)} copy(bf16[1,2400,512]{2,1,0:T(8,128)(2,1)S(1)} %fusion.8) | data formatting | bytes 4915200 | tf_op jit(solution)/shard_map/convert_element_type | solution.py:153
  310.9 16.3 %reduce.10 = bf16[2400,512]{1,0:T(8,128)(2,1)S(1)} reduce(bf16[2400,1,512]{2,1,0:T(2,128)(2,1)} %bitcast.108, bf16[]{:T(256)} %broadcast.269), dimensions={1}, to_apply=%bitcast.100.reduce_sub_computation | reduce | bytes 4915202
  329.6 5.7 all-to-all-done.1
  335.3 4.5 all-to-all-start.3
  340.0 5.5 reshape.435
  345.5 3.1 copy.146
  348.6 4.7 gather_fusion
  353.3 4.0 reshape.385
  357.3 7.2 %multiply_reduce_fusion.1 = (f32[600,2]{1,0:T(8,128)S(1)}, f32[600,512]{1,0:T(8,128)}) fusion(f32[600,2,512]{2,1,0:T(2,128)} %reshape.385, f32[600,512]{1,0:T(8,128)S(1)} %copy-done.5, f32[600,2]{1,0:T(8,128)S(1)} %copy.113), kind=kLoop, calls=%fused_computation.33 | loop fusion | flops 2149200 | bytes 4924800 | tf_op jit(solution)/shard_map/reduce_sum | solution.py:141
  364.7 30.7 %all-to-all-done.3 = bf16[4,2,153600]{2,1,0:T(2,128)(2,1)} async-done(((bf16[4,2,153600]{2,1,0:T(2,128)(2,1)}), bf16[4,2,153600]{2,1,0:T(2,128)(2,1)}, u32[]{:S(2)}, u32[]{:S(2)}) %all-to-all-start.3) | async-done | bytes 2457632 | tf_op jit(solution)/shard_map/all_to_all | solution.py:156
  395.4 5.3 reshape.437
  400.7 3.1 copy.145
  403.8 4.7 gather_fusion.1
  408.5 4.1 reshape.388
  412.6 4.7 reduce_sum.196
  423.3 4.5 multiply_reduce_fusion
  430.7 3.7 multiply_convert_fusion.1
  442.2 10.2 %fusion.10 = bf16[1,512,2048]{2,1,0:T(8,128)(2,1)} fusion(bf16[2400,512]{1,0:T(8,128)(2,1)} %bitcast.6, bf16[2400,2048]{1,0:T(8,128)(2,1)} %get-tuple-element.28), kind=kOutput, calls=%fused_computation.29 | convolution fusion | flops 5034213376 | bytes 14385152 | tf_op jit(solution)/shard_map/erd,erf->edf/dot_general | solution.py:152
  452.5 10.0 %fusion.11 = bf16[1,2048,512]{2,1,0:T(8,128)(2,1)} fusion(bf16[2400,2048]{1,0:T(8,128)(2,1)} %copy-done.36, bf16[2400,512]{1,0:T(8,128)(2,1)} %bitcast.11), kind=kOutput, calls=%fused_computation.30 | convolution fusion | flops 5034213376 | bytes 14385152 | tf_op jit(solution)/shard_map/erf,erd->efd/dot_general | solution.py:149
  477.7 4.9 fusion.30
  482.6 67.8 %all-reduce.13.cloned.1.call-done = (bf16[1,512,2048]{2,1,0:T(8,128)(2,1)}, bf16[1,2048,512]{2,1,0:T(8,128)(2,1)}) async-done(((bf16[1,512,2048]{2,1,0:T(8,128)(2,1)}, bf16[1,2048,512]{2,1,0:T(8,128)(2,1)}), (bf16[1,512,2048]{2,1,0:T(8,128)(2,1)}, bf16[1,2048,512]{2,1,0:T(8,128)(2,1)})) %all-reduce.13.cloned.1.call-update) | async-done | bytes 4194320 | tf_op jit(solution)/shard_map/psum | solution.py:215
  550.5 4.3 convert_element_type.197
  559.7 3.5 multiply_reduce_fusion.5
  564.9 39.8 %all-reduce.3 = (f32[512]{0:T(512)}, f32[512]{0:T(512)}, f32[512,4]{0,1:T(4,128)}) all-reduce(f32[512]{0:T(512)S(1)} %get-tuple-element.11, f32[512]{0:T(512)S(1)} %get-tuple-element.9, f32[512,4]{0,1:T(4,128)S(1)} %fusion.51), channel_id=1, replica_groups=mesh['dp'=4,'ctx'=2,'expert'=4] {'dp','ctx','expert'}, use_global_device_ids=true, to_apply=%region_26.27 | all-reduce | flops 3072 | bytes 24576 | tf_op jit(solution)/shard_map/psum | solution.py:211
  604.7 95.5 %all-reduce.11.cloned.1.call-done = (f32[512,1536]{1,0:T(8,128)}, f32[512,512]{1,0:T(8,128)}) async-done(((f32[512,1536]{1,0:T(8,128)}, f32[512,512]{1,0:T(8,128)}), (f32[512,1536]{1,0:T(8,128)}, f32[512,512]{1,0:T(8,128)})) %all-reduce.11.cloned.1.call-update) | async-done | bytes 4194320 | tf_op jit(solution)/shard_map/psum | solution.py:211
  700.2 3.9 copy.156
  (176 shorter events, 70.8 us)
Async XLA Ops:
  7.2 193.6 %copy-start = (bf16[1,512,2048]{2,1,0:T(8,128)(2,1)S(1)}, bf16[1,512,2048]{2,1,0:T(8,128)(2,1)}, u32[]{:S(2)}) copy-start(bf16[1,512,2048]{2,1,0:T(8,128)(2,1)} %param.17) | copy-start | bytes 6291460
  7.2 5.3 copy-start.32
  7.2 28.9 %all-gather.5.cloned.1.call-start = ((), (), s32[]{:S(2)}) async-start(), calls=%async_computation.5 | async-start | bytes 2457600 | tf_op jit(solution)/shard_map/all_gather | solution.py:34
  9.8 6.5 copy-start.9
  11.8 4.5 copy-start.26
  11.9 4.5 copy-start.23
  11.9 0.6 copy-start.28
  21.6 2.7 copy-start.22
  22.8 26.0 %all-gather.3.cloned.1.call-start = ((), (), s32[]{:S(2)}) async-start(), calls=%async_computation.4 | async-start | bytes 2457600 | tf_op jit(solution)/shard_map/all_gather | solution.py:35
  29.4 6.6 copy-start.4
  31.7 4.4 copy-start.31
  36.0 4.1 copy-start.16
  56.7 4.1 copy-start.10
  60.7 2.9 copy-start.25
  62.6 1.1 copy-start.2
  62.6 1.3 copy-start.30
  63.9 20.0 %copy-start.12 = (bf16[600,512]{1,0:T(8,128)(2,1)}, bf16[600,512]{1,0:T(8,128)(2,1)S(1)}, u32[]{:S(2)}) copy-start(bf16[600,512]{1,0:T(8,128)(2,1)S(1)} %multiply_convert_fusion.6) | copy-start | bytes 1843204
  79.0 61.3 %all-to-all-start.2 = ((bf16[4,600,512]{2,1,0:T(8,128)(2,1)}), bf16[4,600,512]{2,1,0:T(8,128)(2,1)}, u32[]{:S(2)}, u32[]{:S(2)}) async-start(bf16[4,600,512]{2,1,0:T(8,128)(2,1)} %bitcast.109), calls=%async_computation.2 | async-start | bytes 4915200 | tf_op jit(solution)/shard_map/all_to_all | solution.py:147
  140.4 60.4 %all-to-all-start = ((bf16[4,600,512]{2,1,0:T(8,128)(2,1)}), bf16[4,600,512]{2,1,0:T(8,128)(2,1)}, u32[]{:S(2)}, u32[]{:S(2)}) async-start(bf16[4,600,512]{2,1,0:T(8,128)(2,1)} %bitcast.110), calls=%async_computation | async-start | bytes 4915200 | tf_op jit(solution)/shard_map/all_to_all | solution.py:70
  200.8 24.4 %copy-start.34 = (bf16[1,2048,512]{2,1,0:T(8,128)(2,1)S(1)}, bf16[1,2048,512]{2,1,0:T(8,128)(2,1)}, u32[]{:S(2)}) copy-start(bf16[1,2048,512]{2,1,0:T(8,128)(2,1)} %param.18) | copy-start | bytes 6291460
  225.2 5.5 copy-start.36
  274.9 60.4 %all-to-all-start.1 = ((bf16[4,2,153600]{2,1,0:T(2,128)(2,1)}), bf16[4,2,153600]{2,1,0:T(2,128)(2,1)}, u32[]{:S(2)}, u32[]{:S(2)}) async-start(bf16[4,2,153600]{2,1,0:T(2,128)(2,1)} %reshape.434), calls=%async_computation.1 | async-start | bytes 4915200 | tf_op jit(solution)/shard_map/all_to_all | solution.py:76
  335.3 60.0 %all-to-all-start.3 = ((bf16[4,2,153600]{2,1,0:T(2,128)(2,1)}), bf16[4,2,153600]{2,1,0:T(2,128)(2,1)}, u32[]{:S(2)}, u32[]{:S(2)}) async-start(bf16[4,2,153600]{2,1,0:T(2,128)(2,1)} %reshape.436), calls=%async_computation.3 | async-start | bytes 4915200 | tf_op jit(solution)/shard_map/all_to_all | solution.py:156
  339.9 130.6 %all-reduce.15.cloned.1.call-start = ((), (), s32[]{:S(2)}) async-start(), calls=%async_computation.8 | async-start | bytes 4915200
  353.3 4.0 copy-start.5
  412.6 4.7 copy-start.3
  417.3 1.3 copy-start.15
  418.6 1.4 copy-start.6
  420.0 1.3 copy-start.19
  420.2 1.1 copy-start.7
  421.2 6.6 slice-start
  423.3 4.6 slice-start.1
  430.7 3.7 copy-start.17
  442.2 108.3 %all-reduce.13.cloned.1.call-start = ((), (), s32[]{:S(2)}) async-start(), calls=%async_computation.7 | async-start | bytes 8388608 | tf_op jit(solution)/shard_map/psum | solution.py:215
  462.4 0.7 copy-start.35
  462.4 237.8 %all-reduce.11.cloned.1.call-start = ((), (), s32[]{:S(2)}) async-start(), calls=%async_computation.6 | async-start | bytes 8388608 | tf_op jit(solution)/shard_map/psum | solution.py:211
  466.8 2.2 copy-start.8
  466.8 2.2 copy-start.14
  473.1 4.6 copy-start.11
  473.1 4.6 copy-start.27
  473.1 4.6 copy-start.29
  473.1 4.6 copy-start.33
  477.7 4.9 copy-start.21
  550.5 4.3 copy-start.18
  554.7 4.6 copy-start.13
  559.7 3.6 copy-start.24
  700.2 3.9 copy-start.20
  700.2 4.9 copy-start.1
Sparse Core Ops, SparseCore 0:
  22.9 12.5 all-gather.4
  37.6 11.0 all-gather.2
  442.3 21.3 all-reduce.14
  468.0 82.3 all-reduce.12
  557.5 142.6 all-reduce.10
where the time goes:
time: 716 us; the launch traced here: 712 us
  waiting for transfers between devices  287 us (40%)
  local copies, waits for them, and re-layouts  160 us (22%)
  matrix products  112 us (16%)
  other arithmetic  78.6 us (11%)
  blocking collectives  39.8 us (6%)
  starting transfers between devices  19.8 us (3%)
  between operations  15.4 us (2%)
    psum x1, waiting for transfers between devices, shards(): lax.psum((grad_gain_one, grad_qkv, grad_out, grad_gain_two, grad_router),...  95.5 us
    psum x1, waiting for transfers between devices, shards(): lax.psum(grad_in.astype(jnp.bfloat16), ('dp', 'ctx')).astype(jnp.float32)  67.8 us
    all_to_all x1, waiting for transfers between devices, forward(): lax.all_to_all(buffer, 'expert', split_axis=0, concat_axis=1, tiled=True)  44.1 us
    all_to_all x1, waiting for transfers between devices, shards(): lax.all_to_all(grad_buffer, 'expert', split_axis=0, concat_axis=1, tiled=...  40.7 us
    psum x1, blocking collectives, shards(): lax.psum((grad_gain_one, grad_qkv, grad_out, grad_gain_two, grad_router),...  39.8 us
    unnamed x94, local copies, waits for them, and re-layouts  36.9 us
    unnamed x4, other arithmetic  34.1 us
    all_to_all x1, waiting for transfers between devices, shards(): lax.all_to_all(d_in, 'expert', split_axis=1, concat_axis=0, tiled=True)  30.7 us
  transfers between devices with their start and end apart: 9, of which 7 were waited for; matrix products, arithmetic and copies ran while one was open for 25% of the time, Pallas kernels for 0%

commit v1 on v0

--- a/solution.py
+++ b/solution.py
@@ -212,7 +212,7 @@
         (grad_gain_one, grad_qkv, grad_out, grad_gain_two, grad_router), ("dp", "ctx", "expert")
     )
     grad_in, grad_back = (
-        lax.psum(grad_in.astype(jnp.bfloat16), ("dp", "ctx")).astype(jnp.float32),
+        jax.lax.psum(jax.lax.psum(grad_in.astype(jnp.bfloat16), "ctx"), "dp").astype(jnp.float32),
         lax.psum(grad_back.astype(jnp.bfloat16), ("dp", "ctx")).astype(jnp.float32),
     )
     return (

time: 716 us -> 776 us (1.084)
  waiting for transfers between devices: 287 us -> 345 us
    psum x1, waiting for transfers between devices: 95.5 us -> 144 us  [shards(): lax.psum((grad_gain_one, grad_qkv, grad_out, grad_gain_two, grad_router),...]
    unnamed x6 -> x7, waiting for transfers between devices: 0.08 us -> 18.5 us
    all_to_all x1, waiting for transfers between devices: 30.7 us -> 20.5 us  [shards(): lax.all_to_all(d_in, 'expert', split_axis=1, concat_axis=0, tiled=True)]
    unnamed x94 -> x96, local copies, waits for them, and re-layouts: 36.9 us -> 35.3 us
    psum x1 -> x2, waiting for transfers between devices: 67.8 us -> 69.1 us  [the longest x1 47.7 us: shards(): lax.psum(grad_back.astype(jnp.bfloat16), ('dp', 'ctx')).astype(jnp.float32)]
  transfers between devices with their start and end apart: 9 -> 10, of which waited for: 7 -> 9; matrix products, arithmetic and copies ran while one was open for 25% -> 23% of each run, Pallas kernels for 0% -> 0%
where the time goes in v1:
time: 776 us; the launch traced here: 771 us
  waiting for transfers between devices  345 us (44%)
  local copies, waits for them, and re-layouts  158 us (20%)
  matrix products  113 us (15%)
  other arithmetic  80.4 us (10%)
  blocking collectives  39.4 us (5%)
  starting transfers between devices  19.4 us (2%)
  between operations  15.7 us (2%)
    psum x1, waiting for transfers between devices, shards(): lax.psum((grad_gain_one, grad_qkv, grad_out, grad_gain_two, grad_router),...  144 us
    psum x1, waiting for transfers between devices, shards(): lax.psum(grad_back.astype(jnp.bfloat16), ('dp', 'ctx')).astype(jnp.float32)  47.7 us
    all_to_all x1, waiting for transfers between devices, forward(): lax.all_to_all(buffer, 'expert', split_axis=0, concat_axis=1, tiled=True)  44.2 us
    all_to_all x1, waiting for transfers between devices, shards(): lax.all_to_all(grad_buffer, 'expert', split_axis=0, concat_axis=1, tiled=...  40.7 us
    psum x1, blocking collectives, shards(): lax.psum((grad_gain_one, grad_qkv, grad_out, grad_gain_two, grad_router),...  39.4 us
    unnamed x96, local copies, waits for them, and re-layouts  35.3 us
    unnamed x4, other arithmetic  34.1 us
    dot_general x1, matrix products, forward(): jnp.einsum('erd,edf->erf', arrived, w_in, preferred_element_type=jnp.floa...  24.4 us
  transfers between devices with their start and end apart: 10, of which 9 were waited for; matrix products, arithmetic and copies ran while one was open for 23% of the time, Pallas kernels for 0%

profile of v1, /device:TPU:0, one launch (start us, length us, event | category | flops | bytes accessed | tf_op | source)
XLA Modules:
  0.0 771.2 jit_solution(15100873590402025199)
XLA Ops:
  12.5 3.8 convolution_convert_fusion.2
  16.4 3.7 reshape.366
  31.5 4.3 mul.324
  36.0 4.0 copy.110
  40.0 6.3 fusion.48
  48.7 4.0 copy.107
  52.7 3.9 fusion.22
  64.7 14.7 %scatter_custom_fusion.1 = bf16[2400,512]{1,0:T(8,128)(2,1)} fusion(s32[1200]{0:T(1024)S(1)} %fusion.39, f32[1200,512]{1,0:T(8,128)} %mul.324, f32[1200]{0:T(1024)S(1)} %div.90, bf16[]{:T(256)} %constant.40.clone.1), kind=kCustom, calls=%fused_computation.58 | custom fusion | flops 1228800 | bytes 4923394 | tf_op jit(solution)/shard_map/scatter | solution.py:145
  79.4 4.9 all-to-all-start.2
  85.9 3.9 reshape.409
  89.8 10.2 %scatter_custom_fusion = bf16[2400,512]{1,0:T(8,128)(2,1)} fusion(s32[1200]{0:T(1024)S(1)} %fusion.39, bf16[1200,512]{1,0:T(8,128)(2,1)} %reshape.409, bf16[]{:T(256)} %constant.40.clone.1), kind=kCustom, calls=%fused_computation.68 | custom fusion | bytes 2458112 | tf_op jit(solution)/shard_map/scatter | solution.py:68
  100.0 40.7 %all-to-all-done.2 = bf16[4,600,512]{2,1,0:T(8,128)(2,1)} async-done(((bf16[4,600,512]{2,1,0:T(8,128)(2,1)}), bf16[4,600,512]{2,1,0:T(8,128)(2,1)}, u32[]{:S(2)}, u32[]{:S(2)}) %all-to-all-start.2) | async-done | bytes 2457632 | tf_op jit(solution)/shard_map/all_to_all | solution.py:147
  140.7 4.7 all-to-all-start
  145.5 11.4 %fusion.15 = f32[2400,2048]{1,0:T(8,128)} fusion(bf16[2400,512]{1,0:T(8,128)(2,1)} %bitcast.11, bf16[1,2048,512]{2,1,0:T(8,128)(2,1)} %param.18), kind=kOutput, calls=%fused_computation.40 | convolution fusion | flops 5033164800 | bytes 24215552 | tf_op jit(solution)/shard_map/erd,efd->erf/dot_general | solution.py:148
  156.9 44.2 %all-to-all-done = bf16[4,600,512]{2,1,0:T(8,128)(2,1)} async-done(((bf16[4,600,512]{2,1,0:T(8,128)(2,1)}), bf16[4,600,512]{2,1,0:T(8,128)(2,1)}, u32[]{:S(2)}, u32[]{:S(2)}) %all-to-all-start) | async-done | bytes 2457632 | tf_op jit(solution)/shard_map/all_to_all | solution.py:70
  201.1 24.4 %fusion.4 = (bf16[2400,2048]{1,0:T(8,128)(2,1)}, bf16[2400,2048]{1,0:T(8,128)(2,1)S(1)}) fusion(f32[2400,2048]{1,0:T(8,128)} %fusion.15, bf16[2400,512]{1,0:T(8,128)(2,1)} %bitcast.6, bf16[1,512,2048]{2,1,0:T(8,128)(2,1)S(1)} %copy-done), kind=kOutput, calls=%fused_computation.12 | convolution fusion | flops 5160960000 | bytes 43876352 | tf_op jit(solution)/shard_map/erd,edf->erf/dot_general | solution.py:71
  225.5 5.5 fusion.7
  231.0 21.7 %copy.149 = bf16[1,2400,512]{2,0,1:T(2,128)(2,1)} copy(bf16[1,2400,512]{2,1,0:T(8,128)(2,1)S(1)} %fusion.7) | data formatting | bytes 4915200 | tf_op jit(solution)/shard_map/convert_element_type | solution.py:73
  253.2 17.7 %reduce.11 = bf16[2400,512]{1,0:T(8,128)(2,1)} reduce(bf16[2400,1,512]{2,1,0:T(2,128)(2,1)} %bitcast.107, bf16[]{:T(256)} %broadcast.269), dimensions={1}, to_apply=%bitcast.101.reduce_sub_computation | reduce | bytes 4915202
  270.9 4.3 reshape.434
  275.2 4.8 all-to-all-start.1
  280.0 9.4 %fusion.8 = bf16[1,2400,512]{2,1,0:T(8,128)(2,1)S(1)} fusion(bf16[2400,2048]{1,0:T(8,128)(2,1)} %get-tuple-element.27, bf16[1,512,2048]{2,1,0:T(8,128)(2,1)S(1)} %copy-done), kind=kOutput, calls=%fused_computation.23 | convolution fusion | flops 5034393600 | bytes 14385152 | tf_op jit(solution)/shard_map/erf,edf->erd/dot_general | solution.py:153
  289.4 21.7 %copy.148 = bf16[1,2400,512]{2,0,1:T(2,128)(2,1)} copy(bf16[1,2400,512]{2,1,0:T(8,128)(2,1)S(1)} %fusion.8) | data formatting | bytes 4915200 | tf_op jit(solution)/shard_map/convert_element_type | solution.py:153
  311.0 16.3 %reduce.10 = bf16[2400,512]{1,0:T(8,128)(2,1)S(1)} reduce(bf16[2400,1,512]{2,1,0:T(2,128)(2,1)} %bitcast.108, bf16[]{:T(256)} %broadcast.269), dimensions={1}, to_apply=%bitcast.100.reduce_sub_computation | reduce | bytes 4915202
  329.8 5.7 all-to-all-done.1
  335.5 4.5 all-to-all-start.3
  340.1 10.4 %fusion.10 = bf16[1,512,2048]{2,1,0:T(8,128)(2,1)} fusion(bf16[2400,512]{1,0:T(8,128)(2,1)} %bitcast.6, bf16[2400,2048]{1,0:T(8,128)(2,1)} %get-tuple-element.27), kind=kOutput, calls=%fused_computation.29 | convolution fusion | flops 5034213376 | bytes 14385152 | tf_op jit(solution)/shard_map/erd,erf->edf/dot_general | solution.py:152
  350.5 5.3 reshape.435
  358.9 4.7 gather_fusion
  363.6 4.0 reshape.385
  367.6 7.2 multiply_reduce_fusion.1
  375.0 20.5 %all-to-all-done.3 = bf16[4,2,153600]{2,1,0:T(2,128)(2,1)} async-done(((bf16[4,2,153600]{2,1,0:T(2,128)(2,1)}), bf16[4,2,153600]{2,1,0:T(2,128)(2,1)}, u32[]{:S(2)}, u32[]{:S(2)}) %all-to-all-start.3) | async-done | bytes 2457632 | tf_op jit(solution)/shard_map/all_to_all | solution.py:156
  395.5 5.3 reshape.437
  404.0 4.7 gather_fusion.1
  408.6 4.0 reshape.388
  412.7 4.7 reduce_sum.196
  423.4 4.5 multiply_reduce_fusion
  442.4 10.2 %fusion.11 = bf16[1,2048,512]{2,1,0:T(8,128)(2,1)} fusion(bf16[2400,2048]{1,0:T(8,128)(2,1)} %copy-done.37, bf16[2400,512]{1,0:T(8,128)(2,1)} %bitcast.11), kind=kOutput, calls=%fused_computation.30 | convolution fusion | flops 5034213376 | bytes 14385152 | tf_op jit(solution)/shard_map/erf,erd->efd/dot_general | solution.py:149
  452.7 18.4 %all-reduce.17.cloned.1.call-done = (bf16[6,200,512]{2,1,0:T(8,128)(2,1)}, bf16[6,200,512]{2,1,0:T(8,128)(2,1)}, bf16[1,512,2048]{2,1,0:T(8,128)(2,1)}) async-done(((bf16[6,200,512]{2,1,0:T(8,128)(2,1)}, bf16[6,200,512]{2,1,0:T(8,128)(2,1)}, bf16[1,512,2048]{2,1,0:T(8,128)(2,1)}), (bf16[6,200,512]{2,1,0:T(8,128)(2,1)}, bf16[6,200,512]{2,1,0:T(8,128)(2,1)}, ...) | async-done | bytes 4554768
  485.1 4.9 fusion.30
  490.0 47.7 %all-reduce.13.cloned.1.call-done = bf16[1,2048,512]{2,1,0:T(8,128)(2,1)} async-done(((bf16[1,2048,512]{2,1,0:T(8,128)(2,1)}), bf16[1,2048,512]{2,1,0:T(8,128)(2,1)}) %all-reduce.13.cloned.1.call-update) | async-done | bytes 2097168 | tf_op jit(solution)/shard_map/psum | solution.py:216
  537.8 4.2 convert_element_type.200
  544.3 4.2 multiply_reduce_fusion.5
  550.2 39.4 %all-reduce.3 = (f32[512]{0:T(512)}, f32[512]{0:T(512)}, f32[512,4]{0,1:T(4,128)}) all-reduce(f32[512]{0:T(512)S(1)} %get-tuple-element.11, f32[512]{0:T(512)S(1)} %get-tuple-element.9, f32[512,4]{0,1:T(4,128)S(1)} %fusion.51), channel_id=1, replica_groups=mesh['dp'=4,'ctx'=2,'expert'=4] {'dp','ctx','expert'}, use_global_device_ids=true, to_apply=%region_26.27 | all-reduce | flops 3072 | bytes 24576 | tf_op jit(solution)/shard_map/psum | solution.py:211
  589.6 21.3 %all-reduce.11.cloned.1.call-done = bf16[1,512,2048]{2,1,0:T(8,128)(2,1)} async-done(((bf16[1,512,2048]{2,1,0:T(8,128)(2,1)}), bf16[1,512,2048]{2,1,0:T(8,128)(2,1)}) %all-reduce.11.cloned.1.call-update) | async-done | bytes 2097168 | tf_op jit(solution)/shard_map/psum | solution.py:215
  611.0 4.1 convert_element_type.197
  615.1 144.1 %all-reduce.15.cloned.1.call-done = (f32[512,1536]{1,0:T(8,128)}, f32[512,512]{1,0:T(8,128)}) async-done(((f32[512,1536]{1,0:T(8,128)}, f32[512,512]{1,0:T(8,128)}), (f32[512,1536]{1,0:T(8,128)}, f32[512,512]{1,0:T(8,128)})) %all-reduce.15.cloned.1.call-update) | async-done | bytes 4194320 | tf_op jit(solution)/shard_map/psum | solution.py:211
  759.2 3.9 copy.157
  (181 shorter events, 76.7 us)
Async XLA Ops:
  7.2 193.9 %copy-start = (bf16[1,512,2048]{2,1,0:T(8,128)(2,1)S(1)}, bf16[1,512,2048]{2,1,0:T(8,128)(2,1)}, u32[]{:S(2)}) copy-start(bf16[1,512,2048]{2,1,0:T(8,128)(2,1)} %param.17) | copy-start | bytes 6291460
  7.2 5.3 copy-start.33
  7.2 28.8 %all-gather.5.cloned.1.call-start = ((), (), s32[]{:S(2)}) async-start(), calls=%async_computation.5 | async-start | bytes 2457600 | tf_op jit(solution)/shard_map/all_gather | solution.py:34
  9.8 6.5 copy-start.9
  11.8 4.5 copy-start.27
  11.9 4.5 copy-start.24
  21.6 2.6 copy-start.23
  22.8 26.0 %all-gather.3.cloned.1.call-start = ((), (), s32[]{:S(2)}) async-start(), calls=%async_computation.4 | async-start | bytes 2457600 | tf_op jit(solution)/shard_map/all_gather | solution.py:35
  29.2 6.6 copy-start.4
  31.5 4.4 copy-start.32
  35.9 4.1 copy-start.16
  56.7 4.1 copy-start.10
  60.8 2.9 copy-start.26
  62.7 1.3 copy-start.31
  63.9 20.3 %copy-start.12 = (bf16[600,512]{1,0:T(8,128)(2,1)}, bf16[600,512]{1,0:T(8,128)(2,1)S(1)}, u32[]{:S(2)}) copy-start(bf16[600,512]{1,0:T(8,128)(2,1)S(1)} %multiply_convert_fusion.6) | copy-start | bytes 1843204
  79.4 61.4 %all-to-all-start.2 = ((bf16[4,600,512]{2,1,0:T(8,128)(2,1)}), bf16[4,600,512]{2,1,0:T(8,128)(2,1)}, u32[]{:S(2)}, u32[]{:S(2)}) async-start(bf16[4,600,512]{2,1,0:T(8,128)(2,1)} %bitcast.109), calls=%async_computation.2 | async-start | bytes 4915200 | tf_op jit(solution)/shard_map/all_to_all | solution.py:147
  140.7 60.3 %all-to-all-start = ((bf16[4,600,512]{2,1,0:T(8,128)(2,1)}), bf16[4,600,512]{2,1,0:T(8,128)(2,1)}, u32[]{:S(2)}, u32[]{:S(2)}) async-start(bf16[4,600,512]{2,1,0:T(8,128)(2,1)} %bitcast.110), calls=%async_computation | async-start | bytes 4915200 | tf_op jit(solution)/shard_map/all_to_all | solution.py:70
  201.1 24.4 %copy-start.35 = (bf16[1,2048,512]{2,1,0:T(8,128)(2,1)S(1)}, bf16[1,2048,512]{2,1,0:T(8,128)(2,1)}, u32[]{:S(2)}) copy-start(bf16[1,2048,512]{2,1,0:T(8,128)(2,1)} %param.18) | copy-start | bytes 6291460
  225.5 5.5 copy-start.37
  275.2 60.2 %all-to-all-start.1 = ((bf16[4,2,153600]{2,1,0:T(2,128)(2,1)}), bf16[4,2,153600]{2,1,0:T(2,128)(2,1)}, u32[]{:S(2)}, u32[]{:S(2)}) async-start(bf16[4,2,153600]{2,1,0:T(2,128)(2,1)} %reshape.434), calls=%async_computation.1 | async-start | bytes 4915200 | tf_op jit(solution)/shard_map/all_to_all | solution.py:76
  335.5 60.0 %all-to-all-start.3 = ((bf16[4,2,153600]{2,1,0:T(2,128)(2,1)}), bf16[4,2,153600]{2,1,0:T(2,128)(2,1)}, u32[]{:S(2)}, u32[]{:S(2)}) async-start(bf16[4,2,153600]{2,1,0:T(2,128)(2,1)} %reshape.436), calls=%async_computation.3 | async-start | bytes 4915200 | tf_op jit(solution)/shard_map/all_to_all | solution.py:156
  340.0 131.1 %all-reduce.17.cloned.1.call-start = ((), (), s32[]{:S(2)}) async-start(), calls=%async_computation.9 | async-start | bytes 9109504
  363.6 4.0 copy-start.5
  412.7 4.7 copy-start.3
  417.4 1.3 copy-start.15
  418.7 1.4 copy-start.6
  420.1 1.3 copy-start.18
  420.3 1.1 copy-start.7
  421.4 6.6 slice-start
  423.4 4.6 slice-start.1
  430.8 3.7 copy-start.17
  442.4 95.4 %all-reduce.13.cloned.1.call-start = ((), (), s32[]{:S(2)}) async-start(), calls=%async_computation.7 | async-start | bytes 4194304 | tf_op jit(solution)/shard_map/psum | solution.py:216
  452.6 18.6 %copy-start.36 = (u32[32]{0:T(128)S(1)}, u32[32]{0:T(128)}, u32[]{:S(2)}) copy-start(u32[32]{0:T(128)} %constant.59) | copy-start | bytes 388
  452.7 158.3 %all-reduce.11.cloned.1.call-start = ((), (), s32[]{:S(2)}) async-start(), calls=%async_computation.6 | async-start | bytes 4194304 | tf_op jit(solution)/shard_map/psum | solution.py:215
  471.2 288.0 %all-reduce.15.cloned.1.call-start = ((), (), s32[]{:S(2)}) async-start(), calls=%async_computation.8 | async-start | bytes 8388608 | tf_op jit(solution)/shard_map/psum | solution.py:211
  474.9 2.2 copy-start.8
  474.9 2.2 copy-start.14
  477.1 1.6 copy-start.21
  477.1 2.0 copy-start.22
  480.4 4.6 copy-start.11
  480.4 4.6 copy-start.28
  480.4 4.6 copy-start.30
  480.4 4.6 copy-start.34
  485.1 4.9 copy-start.20
  490.0 54.0 %copy-start.13 = (bf16[600,512]{1,0:T(8,128)(2,1)S(1)}, bf16[600,512]{1,0:T(8,128)(2,1)}, u32[]{:S(2)}) copy-start(bf16[600,512]{1,0:T(8,128)(2,1)} %copy-done.12) | copy-start | bytes 1843204
  544.3 4.2 copy-start.25
  759.2 3.9 copy-start.19
  759.2 4.9 copy-start.1
  (2 other events, 1.6 us)
Sparse Core Ops, SparseCore 0:
  22.9 12.5 all-gather.4
  37.6 11.0 all-gather.2
  442.5 28.6 all-reduce.16
  475.1 62.5 all-reduce.12
  541.0 69.9 all-reduce.10
  617.1 142.0 all-reduce.14
